TPU v7x, 32 devices: a whole 2x2x4 slice. The times are simulated.
32 devices in a mesh: lvl: 4 (over z), sp: 8 (over y, x, core).
Axes of the slice: x: 2, y: 2, z: 4, core: 2. Of those that a mesh axis runs over, the one named last changes fastest.
Arguments:
- input_field: bfloat16 [3, 800, 128, 128], P(None, 'lvl', 'sp'), may hold values from -6 to 6
- cotangent: bfloat16 [3, 800, 128, 128], P(None, 'lvl', 'sp'), may hold values from -6 to 6
- ocean_mask: int32 [3, 128, 128], P(None, 'sp'), may hold values 0 or 1
- crop_rows: int32 [3, 8], P(None, 'sp'), may hold values from 8 to 16, as said below
- step_count: int32 [], replicated, may hold values from 1 to 20
- kernel: float32 [800, 49], P('lvl'), may hold values from -0.875 to 0.875
- kernel_first: float32 [800, 49], P('lvl'), may hold values from -56 to 56
- kernel_second: float32 [800, 49], P('lvl'), may hold values from 7.86432 to 31.45728
- scales: float32 [2, 800], P(None, 'lvl'), may hold values from 0.5 to 1.5
- scales_first: float32 [2, 800], P(None, 'lvl'), may hold values from -56 to 56
- scales_second: float32 [2, 800], P(None, 'lvl'), may hold values from 7.86432 to 31.45728
- expand: float32 [800, 3200], P(None, 'sp'), may hold values from -0.21875 to 0.21875
- expand_first: float32 [800, 3200], P(None, 'sp'), may hold values from -28 to 28
- expand_second: float32 [800, 3200], P(None, 'sp'), may hold values from 1.96608 to 7.86432
- uplift: float32 [3200], P('sp'), may hold values from -1.75 to 1.75
- uplift_first: float32 [3200], P('sp'), may hold values from -28 to 28
- uplift_second: float32 [3200], P('sp'), may hold values from 1.96608 to 7.86432
- shrink: float32 [3200, 800], P('sp'), may hold values from -0.109375 to 0.109375
- shrink_first: float32 [3200, 800], P('sp'), may hold values from -64 to 64
- shrink_second: float32 [3200, 800], P('sp'), may hold values from 9.8304 to 39.3216
- offset: float32 [800], P('sp'), may hold values from -1.75 to 1.75
- offset_first: float32 [800], P('sp'), may hold values from -112 to 112
- offset_second: float32 [800], P('sp'), may hold values from 27.52512 to 108.1344
Outputs:
- block_output: float32 [3, 800, 128, 128], P(None, 'lvl', 'sp')
- input_grad: float32 [3, 800, 128, 128], P(None, 'lvl', 'sp')
- kernel_grad: float32 [800, 49], P('lvl')
- kernel_moment: float32 [800, 49], P('lvl')
- kernel_next: float32 [800, 49], P('lvl')
- scales_grad: float32 [2, 800], P(None, 'lvl')
- scales_moment: float32 [2, 800], P(None, 'lvl')
- scales_next: float32 [2, 800], P(None, 'lvl')
- expand_grad: float32 [800, 3200], P(None, 'sp')
- expand_moment: float32 [800, 3200], P(None, 'sp')
- expand_next: float32 [800, 3200], P(None, 'sp')
- uplift_grad: float32 [3200], P('sp')
- uplift_moment: float32 [3200], P('sp')
- uplift_next: float32 [3200], P('sp')
- shrink_grad: float32 [3200, 800], P('sp')
- shrink_moment: float32 [3200, 800], P('sp')
- shrink_next: float32 [3200, 800], P('sp')
- offset_grad: float32 [800], P('sp')
- offset_moment: float32 [800], P('sp')
- offset_next: float32 [800], P('sp')
- step_next: int32 [], replicated
Inputs may be any that keep to these rules, and one draw needn't show every extreme that they name: `crop_rows`: at least half of a tile's rows; in each micro-batch some tile keeps all 16.
All inputs are finite; a program needn't handle non-finite values. No bound on the sum of `ocean_mask` on one device may be relied on, other than what follows from the above.
Results may differ from a plain program's by a relative error of at most 0.007.
Values may be sent and summed in bfloat16 or wider, within the bound.
A program may use at most 256 MiB of HBM per device.

v0:
```python
import functools
import math

import jax
import jax.numpy as jnp
from jax import lax
from jax.experimental import pallas as pl
from jax.experimental.pallas import tpu as pltpu
from jax.sharding import PartitionSpec as P

KW = 7
MARGIN = KW // 2
GROUP = 8
CLOSE_BLOCK = 40
ROWS = 16

beta_one = 0.9
beta_two = 0.999
epsilon = 1e-08
weight_decay = 0.01
GELU_A = math.sqrt(2.0 / math.pi)
GELU_B = 0.044715


def adamw(weight, first, second, grad, rate, step_float):
    first_new = beta_one * first + (1.0 - beta_one) * grad
    second_new = beta_two * second + (1.0 - beta_two) * grad * grad
    fix_first = 1.0 - jnp.power(beta_one, step_float)
    fix_second = 1.0 - jnp.power(beta_two, step_float)
    update = (
        first_new / fix_first / (jnp.sqrt(second_new / fix_second) + epsilon)
        + weight_decay * weight
    )
    return (second_new, weight - rate * update)


def lane_tap_masks(width):
    lane = lax.broadcasted_iota(jnp.int32, (GROUP, width), 1)
    return [
        jnp.logical_and(lane + (b - MARGIN) >= 0, lane + (b - MARGIN) < width)
        for b in range(KW)
    ]


def shifted(value, amount):
    width = value.shape[-1]
    turn = (-amount) % width
    return value if turn == 0 else pltpu.roll(value, turn, 1)


def chip_neighbours(chip):
    across = chip + 1 - 2 * lax.rem(chip, 2)
    along = lax.rem(chip + 2, 4)
    return across, along, lax.rem(across + 2, 4)


def fill_taps(k_ref, taps, masks, groups):
    width = taps.shape[2]

    def fill(g, carry):
        now = pl.ds(pl.multiple_of(g * GROUP, GROUP), GROUP)
        for a in range(KW):
            for b in range(KW):
                t = a * KW + b
                tap = jnp.broadcast_to(k_ref[now, t : t + 1], (GROUP, width))
                taps[t, now, :] = jnp.where(masks[b], tap, 0.0)
        return carry

    lax.fori_loop(0, groups, fill, 0)


def depthwise_rows(source, taps, now, rows, sign):
    width = taps.shape[2]
    outs = [None] * rows
    for first in range(0, rows, 8):
        values = [source(first + r) for r in range(8 + KW - 1)]
        for b in range(KW):
            part = [None] * 8
            for a in range(KW):
                tap = taps[a * KW + b, now, :]
                at = a if sign > 0 else KW - 1 - a
                for i in range(8):
                    term = tap * values[i + at]
                    part[i] = term if part[i] is None else part[i] + term
            for i in range(8):
                moved = shifted(part[i], sign * (b - MARGIN))
                at = first + i
                outs[at] = moved if outs[at] is None else outs[at] + moved
    return outs


def put_columns(columns):
    lane = lax.broadcasted_iota(jnp.int32, (GROUP, 128), 1)
    out = jnp.zeros((GROUP, 128), jnp.float32)
    for at, column in columns:
        out = jnp.where(lane == at, column, out)
    return out


def conv_body(
    crop, x_ref, cot_ref, up_ref, dn_ref, k_ref, mask_ref,
    conv_ref, xt_ref, dres_ref, stat_ref, scr, scc, wscr,
):
    batches, _, height, width = x_ref.shape
    masks = lane_tap_masks(width)
    for a in range(KW):
        for b in range(KW):
            t = a * KW + b
            spread = jnp.broadcast_to(k_ref[:, t : t + 1], (GROUP, width))
            wscr[t] = jnp.where(masks[b], spread, 0.0)

    def one(m, stats):
        for c in range(GROUP):
            scr[c * height : (c + 1) * height, :] = x_ref[m, c].astype(jnp.float32)
            scc[c * height : (c + 1) * height, :] = cot_ref[m, c].astype(jnp.float32)
        limit = crop[m, 0]
        for i in range(height):
            row = scr[pl.ds(i, GROUP, stride=height), :]
            xt_ref[m, MARGIN + i] = jnp.where(i < limit, row, 0.0)
            back = scc[pl.ds(i, GROUP, stride=height), :]
            dres_ref[m, i] = (back * mask_ref[m, i : i + 1, :]).astype(jnp.bfloat16)
        for r in range(MARGIN):
            xt_ref[m, r] = up_ref[m, r].astype(jnp.float32)
            xt_ref[m, MARGIN + height + r] = dn_ref[m, r].astype(jnp.float32)
        total = jnp.zeros((GROUP, width), jnp.float32)
        for base in range(0, height, ROWS):
            acc = [None] * ROWS
            for b in range(KW):
                rolled = [
                    shifted(xt_ref[m, base + r], b - MARGIN) for r in range(ROWS + KW - 1)
                ]
                for a in range(KW):
                    tap = wscr[a * KW + b]
                    for i in range(ROWS):
                        term = tap * rolled[i + a]
                        acc[i] = term if acc[i] is None else acc[i] + term
            for i in range(ROWS):
                conv_ref[m, base + i] = acc[i]
                total = total + acc[i] * mask_ref[m, base + i : base + i + 1, :]
        cells = jnp.sum(mask_ref[m])
        summed = jnp.sum(total, axis=1, keepdims=True)
        mean = summed / jnp.maximum(cells, 1.0)
        spread = jnp.zeros((GROUP, width), jnp.float32)
        for i in range(height):
            off = conv_ref[m, i] - mean
            spread = spread + off * off * mask_ref[m, i : i + 1, :]
        squares = jnp.sum(spread, axis=1, keepdims=True)
        lane = lax.broadcasted_iota(jnp.int32, (GROUP, 128), 1)
        stats = jnp.where(lane == m, summed, stats)
        stats = jnp.where(lane == batches + m, squares, stats)
        return jnp.where(lane == 2 * batches + m, cells, stats)

    stat_ref[...] = lax.fori_loop(0, batches, one, jnp.zeros((GROUP, 128), jnp.float32))


def conv_forward(crop, x, cot, up, down, kernel, mask_cells):
    batches, channels, height, width = x.shape
    groups = pl.cdiv(channels, GROUP)
    natural = pl.BlockSpec((batches, GROUP, height, width), lambda g, c: (0, g, 0, 0))
    turned = lambda rows: pl.BlockSpec((batches, rows, GROUP, width), lambda g, c: (0, 0, g, 0))
    return pl.pallas_call(
        conv_body,
        grid_spec=pltpu.PrefetchScalarGridSpec(
            num_scalar_prefetch=1,
            grid=(groups,),
            in_specs=[
                natural,
                natural,
                turned(MARGIN),
                turned(MARGIN),
                pl.BlockSpec((GROUP, KW * KW), lambda g, c: (g, 0)),
                pl.BlockSpec((batches, height, width), lambda g, c: (0, 0, 0)),
            ],
            out_specs=[
                turned(height),
                turned(height + 2 * MARGIN),
                turned(height),
                pl.BlockSpec((GROUP, 128), lambda g, c: (g, 0)),
            ],
            scratch_shapes=[
                pltpu.VMEM((GROUP * height, width), jnp.float32),
                pltpu.VMEM((GROUP * height, width), jnp.float32),
                pltpu.VMEM((KW * KW, GROUP, width), jnp.float32),
            ],
        ),
        out_shape=[
            jax.ShapeDtypeStruct((batches, height, channels, width), jnp.float32),
            jax.ShapeDtypeStruct((batches, height + 2 * MARGIN, channels, width), jnp.float32),
            jax.ShapeDtypeStruct((batches, height, channels, width), jnp.bfloat16),
            jax.ShapeDtypeStruct((channels, 128), jnp.float32),
        ],
        cost_estimate=pl.CostEstimate(
            flops=2 * KW * KW * batches * channels * height * width,
            bytes_accessed=30 * batches * channels * height * width,
            transcendentals=0,
        ),
    )(crop, x, cot, up, down, kernel, mask_cells)


def forward_body(
    crop, x_hbm, cot_hbm, ocean_ref, kt_ref, scale_ref, et_hbm, w_hbm, up_own, off_own,
    conv_hbm, xt_hbm, norm_hbm, back_hbm, et_all, w_all, par_ref, mask_ref, bias_ref, turned_k,
    xv, cotv, xt, conv, dres, norm, edge, rim, cast, scr, scc, taps, part, stat, msg, srecv, scal, bias, kpad, et_own, w_own,
    load_sem, save_sem, own_sem, pair_send, pair_recv, chip_send, chip_recv,
    b_send, b_recv, s_send, s_recv, h_send, h_recv, d_send, d_recv, d_own,
):
    f32, bf = jnp.float32, jnp.bfloat16
    batches, height, channels, width = conv.shape
    groups = channels // GROUP
    peers, place = lax.axis_size("lvl"), lax.axis_index("lvl")
    spots, spot = lax.axis_size("sp"), lax.axis_index("sp")
    chips = spots // 2
    chip, core = spot // 2, lax.rem(spot, 2)
    sibling = spot + 1 - 2 * core
    rows = height // peers
    mesh_id = pl.DeviceIdType.MESH
    near = chip_neighbours(chip)[:2]

    loads = [
        pltpu.make_async_copy(cot_hbm, cotv, load_sem.at[0]),
        pltpu.make_async_copy(x_hbm, xv, load_sem.at[1]),
    ]
    loads[0].start()
    loads[1].start()

    def own_load(which):
        return pltpu.make_async_copy(
            (et_hbm, w_hbm)[which], (et_own, w_own)[which], load_sem.at[2 + which]
        )

    for which in range(2):
        own_load(which).start()
    barrier = pltpu.get_barrier_semaphore()
    for k in range(1, peers):
        pl.semaphore_signal(
            barrier, inc=1, device_id={"lvl": lax.rem(place + k, peers)}, device_id_type=mesh_id
        )
    for k in range(1, spots):
        pl.semaphore_signal(
            barrier, inc=1, device_id={"sp": lax.rem(spot + k, spots)}, device_id_type=mesh_id
        )

    gathered = (et_all, w_all)

    def own_copy(which):
        return pltpu.make_async_copy(cast.at[which], gathered[which].at[spot], own_sem.at[which])

    def pair_copy(which):
        return pltpu.make_async_remote_copy(
            src_ref=cast.at[which], dst_ref=gathered[which].at[spot],
            send_sem=pair_send.at[which], recv_sem=pair_recv.at[which],
            device_id={"sp": sibling}, device_id_type=mesh_id,
        )

    def chip_copy(which, k):
        to = 2 * near[k] + core
        return pltpu.make_async_remote_copy(
            src_ref=cast.at[which], dst_ref=gathered[which].at[spot],
            send_sem=chip_send.at[which, k], recv_sem=chip_recv.at[which, k],
            device_id={"sp": to}, device_id_type=mesh_id,
        )

    def bias_copy(k):
        return pltpu.make_async_remote_copy(
            src_ref=bias, dst_ref=bias_ref.at[spot],
            send_sem=b_send.at[k], recv_sem=b_recv.at[k],
            device_id={"sp": lax.rem(spot + k, spots)}, device_id_type=mesh_id,
        )

    def stat_copy(k):
        return pltpu.make_async_remote_copy(
            src_ref=msg, dst_ref=srecv.at[k], send_sem=s_send.at[k], recv_sem=s_recv.at[k],
            device_id={"sp": lax.rem(spot + k, spots)}, device_id_type=mesh_id,
        )

    def to_next():
        return pltpu.make_async_remote_copy(
            src_ref=edge.at[1], dst_ref=rim.at[0], send_sem=h_send.at[0], recv_sem=h_recv.at[0],
            device_id={"sp": lax.rem(spot + 1, spots)}, device_id_type=mesh_id,
        )

    def to_prev():
        return pltpu.make_async_remote_copy(
            src_ref=edge.at[0], dst_ref=rim.at[1], send_sem=h_send.at[1], recv_sem=h_recv.at[1],
            device_id={"sp": lax.rem(spot + spots - 1, spots)}, device_id_type=mesh_id,
        )

    span = pl.ds(pl.multiple_of(place * channels, 8), channels)

    def dres_copy(k):
        to = lax.rem(place + k, peers)
        return pltpu.make_async_remote_copy(
            src_ref=dres.at[:, pl.ds(to * rows, rows)], dst_ref=back_hbm.at[:, :, span, :],
            send_sem=d_send.at[k], recv_sem=d_recv.at[k],
            device_id={"lvl": to}, device_id_type=mesh_id,
        )

    def dres_own():
        return pltpu.make_async_copy(
            dres.at[:, pl.ds(place * rows, rows)], back_hbm.at[:, :, span, :], d_own.at[0]
        )

    row = lax.broadcasted_iota(jnp.int32, (height, width), 0)
    for m in range(batches):
        keep = (row < crop[m]).astype(f32)
        mask_ref[m] = ocean_ref[m].astype(f32) * keep

    def turn_cot(g, carry):
        c0 = pl.multiple_of(g * GROUP, GROUP)
        now = pl.ds(c0, GROUP)
        for m in range(batches):
            for c in range(GROUP):
                scc[m, c * height : (c + 1) * height, :] = cotv[m, c0 + c].astype(f32) * mask_ref[m]
            for i in range(height):
                dres[m, i, now, :] = scc[m, pl.ds(i, GROUP, stride=height), :].astype(bf)
        return carry

    def turn_x(g, carry):
        c0 = pl.multiple_of(g * GROUP, GROUP)
        now = pl.ds(c0, GROUP)
        for m in range(batches):
            keep = (row < crop[m]).astype(f32)
            for c in range(GROUP):
                scr[m, c * height : (c + 1) * height, :] = xv[m, c0 + c].astype(f32) * keep
            for i in range(height):
                value = scr[m, pl.ds(i, GROUP, stride=height), :]
                xt[m, MARGIN + i, now, :] = value
                if i < MARGIN:
                    edge[0, m, i, now, :] = value.astype(bf)
                if i >= height - MARGIN:
                    edge[1, m, i - (height - MARGIN), now, :] = value.astype(bf)
        return carry

    loads[0].wait()
    lax.fori_loop(0, groups, turn_cot, 0)
    pl.semaphore_wait(barrier, peers - 1 + spots - 1)
    for k in range(1, peers):
        dres_copy(k).start()
    dres_own().start()
    loads[1].wait()
    lax.fori_loop(0, groups, turn_x, 0)

    @pl.when(spot < spots - 1)
    def _():
        to_next().start()

    @pl.when(spot > 0)
    def _():
        to_prev().start()

    for which in range(2):
        own_load(which).wait()
    cast[0] = et_own[...].astype(bf)
    cast[1] = w_own[...].astype(bf)
    bias[...] = jnp.zeros_like(bias)
    bias[0:1, : up_own.shape[1]] = up_own[...].astype(bf).astype(f32)
    bias[1:2, : off_own.shape[1]] = off_own[...].astype(bf).astype(f32)
    stat[...] = jnp.zeros_like(stat)
    kpad[...] = jnp.zeros_like(kpad)
    kpad[: KW * KW, :channels] = kt_ref[...]
    turned_k[...] = kpad[...].T
    scal[...] = jnp.zeros_like(scal)
    scal[0:2, :channels] = scale_ref[...]
    bias_ref[spot] = bias[...]
    for k in range(2):
        chip_copy(k, k).start()
    for k in range(2):
        chip_copy(1 - k, k).start()
    for which in range(2):
        pair_copy(which).start()
        own_copy(which).start()
    for k in range(1, spots):
        bias_copy(k).start()
    masks = lane_tap_masks(width)
    fill_taps(turned_k, taps, masks[::-1], groups)

    @pl.when(spot < spots - 1)
    def _():
        to_next().wait_send()
        to_prev().wait_recv()
        xt[:, MARGIN + height :] = rim[1].astype(f32)

    @pl.when(spot > 0)
    def _():
        to_prev().wait_send()
        to_next().wait_recv()
        xt[:, :MARGIN] = rim[0].astype(f32)

    @pl.when(spot == 0)
    def _():
        xt[:, :MARGIN] = jnp.zeros((batches, MARGIN, channels, width), f32)

    @pl.when(spot == spots - 1)
    def _():
        xt[:, MARGIN + height :] = jnp.zeros((batches, MARGIN, channels, width), f32)

    save_x = pltpu.make_async_copy(xt, xt_hbm, save_sem.at[0])
    save_x.start()

    def convolve(g, carry):
        now = pl.ds(pl.multiple_of(g * GROUP, GROUP), GROUP)

        def one(m, inner):
            for base in range(0, height, ROWS):
                outs = depthwise_rows(
                    lambda r: xt[m, base + r, now, :], taps, now, ROWS, 1
                )
                total = None
                for i in range(ROWS):
                    conv[m, base + i, now, :] = outs[i]
                    value = outs[i] * mask_ref[m, base + i : base + i + 1, :]
                    total = value if total is None else total + value
                if base == 0:
                    part[m, now, :] = total
                else:
                    part[m, now, :] += total
            return inner

        lax.fori_loop(0, batches, one, 0)
        return carry

    lax.fori_loop(0, groups, convolve, 0)
    cells = [jnp.sum(mask_ref[m]) for m in range(batches)]
    lane = lax.broadcasted_iota(jnp.int32, (channels, 128), 1)
    tile = jnp.zeros((channels, 128), f32)
    for m in range(batches):
        summed = jnp.sum(part[m], axis=1, keepdims=True)
        tile = jnp.where(lane == m, summed, tile)
        tile = jnp.where(lane == 16 + m, cells[m], tile)
        part[m] = jnp.broadcast_to(summed / jnp.maximum(cells[m], 1.0), (channels, width))

    def scatter(g, carry):
        now = pl.ds(pl.multiple_of(g * GROUP, GROUP), GROUP)
        for m in range(batches):
            mean = part[m, now, :]
            around = None
            for i in range(height):
                off = conv[m, i, now, :] - mean
                value = off * off * mask_ref[m, i : i + 1, :]
                around = value if around is None else around + value
            part[m, now, :] = around
        return carry

    lax.fori_loop(0, groups, scatter, 0)
    for m in range(batches):
        tile = jnp.where(lane == 8 + m, jnp.sum(part[m], axis=1, keepdims=True), tile)
    stat[:channels, :] = tile
    save_conv = pltpu.make_async_copy(conv, conv_hbm, save_sem.at[1])
    save_conv.start()
    msg[...] = stat[...].T[:24, :]
    srecv[0] = msg[...]
    for k in range(1, spots):
        stat_copy(k).start()
    for k in range(1, spots):
        stat_copy(k).wait()
    order = [lax.rem(spot - source + spots, spots) for source in range(spots)]
    summed, count = None, None
    for k in order:
        value, cell = srecv[k, 0:8, :], srecv[k, 16:24, :]
        summed = value if summed is None else summed + value
        count = cell if count is None else count + cell
    count = jnp.maximum(count, 1.0)
    mean = summed / count
    squares = None
    for k in order:
        cell = srecv[k, 16:24, :]
        gap = srecv[k, 0:8, :] / jnp.maximum(cell, 1.0) - mean
        value = srecv[k, 8:16, :] + cell * gap * gap
        squares = value if squares is None else squares + value
    rho = lax.rsqrt(squares / count + 1e-05)
    filler = jnp.zeros((128 - 32, mean.shape[1]), f32)
    par_ref[...] = jnp.concatenate([mean, rho, 1.0 / count, scal[...], filler], axis=0).T

    def normalize(g, carry):
        now = pl.ds(pl.multiple_of(g * GROUP, GROUP), GROUP)
        par = par_ref[now, :]
        gain = jnp.broadcast_to(par[:, 24:25], (GROUP, width))
        shift = jnp.broadcast_to(par[:, 25:26], (GROUP, width))
        for m in range(batches):
            mean = jnp.broadcast_to(par[:, m : m + 1], (GROUP, width))
            rho = jnp.broadcast_to(par[:, 8 + m : 9 + m], (GROUP, width))
            scale = rho * gain
            for i in range(height):
                value = (conv[m, i, now, :] - mean) * scale + shift
                norm[m, i, now, :] = value.astype(bf)
        return carry

    lax.fori_loop(0, groups, normalize, 0)
    save_norm = pltpu.make_async_copy(norm, norm_hbm, save_sem.at[2])
    save_norm.start()
    for k in range(1, spots):
        pltpu.make_async_remote_copy(
            src_ref=bias, dst_ref=bias_ref.at[lax.rem(spot + spots - k, spots)],
            send_sem=b_send.at[k], recv_sem=b_recv.at[k],
            device_id={"sp": lax.rem(spot + k, spots)}, device_id_type=mesh_id,
        ).wait()
    for which in range(2):
        own_copy(which).wait()
        pltpu.make_async_remote_copy(
            src_ref=cast.at[which], dst_ref=gathered[which].at[sibling],
            send_sem=pair_send.at[which], recv_sem=pair_recv.at[which],
            device_id={"sp": sibling}, device_id_type=mesh_id,
        ).wait()
        for k in range(2):
            other = 2 * near[k] + core
            pltpu.make_async_remote_copy(
                src_ref=cast.at[which], dst_ref=gathered[which].at[other],
                send_sem=chip_send.at[which, k], recv_sem=chip_recv.at[which, k],
                device_id={"sp": other}, device_id_type=mesh_id,
            ).wait()
    dres_own().wait()
    for k in range(1, peers):
        source = pl.ds(pl.multiple_of(lax.rem(place + peers - k, peers) * channels, 8), channels)
        pltpu.make_async_remote_copy(
            src_ref=dres.at[:, pl.ds(lax.rem(place + k, peers) * rows, rows)],
            dst_ref=back_hbm.at[:, :, source, :],
            send_sem=d_send.at[k], recv_sem=d_recv.at[k],
            device_id={"lvl": lax.rem(place + k, peers)}, device_id_type=mesh_id,
        ).wait()
    save_x.wait()
    save_conv.wait()
    save_norm.wait()


def forward(crop, x, cot, ocean, kernel, scales, expand_t, shrink, uplift, offset, ident):
    batches, channels, height, width = x.shape
    f32, bf = jnp.float32, jnp.bfloat16
    peers, spots = lax.axis_size("lvl"), lax.axis_size("sp")
    chips = spots // 2
    rows = height // peers
    owned, every = expand_t.shape
    padded = -(-channels // 128) * 128
    lanes = -(-max(owned, offset.shape[1]) // 128) * 128
    hbm = pl.BlockSpec(memory_space=pl.ANY)
    vmem = pl.BlockSpec(memory_space=pltpu.VMEM)
    dma = pltpu.SemaphoreType.DMA
    turned = (batches, height, channels, width)
    framed = (batches, height + 2 * MARGIN, channels, width)
    rim = (2, batches, MARGIN, channels, width)
    V, S = pltpu.VMEM, jax.ShapeDtypeStruct
    return pl.pallas_call(
        forward_body,
        in_specs=[pl.BlockSpec(memory_space=pltpu.SMEM), hbm, hbm, vmem, vmem, vmem, hbm, hbm, vmem, vmem],
        out_specs=[hbm] * 6 + [vmem] * 4,
        out_shape=[
            S(turned, f32), S(framed, f32), S(turned, bf),
            S((batches, rows, every, width), bf),
            S((spots, owned, every), bf), S((spots, owned, every), bf),
            S((padded, 128), f32), S((batches, height, width), f32), S((spots, 8, lanes), f32),
            S((padded, 128), f32),
        ],
        scratch_shapes=[
            V(x.shape, bf), V(x.shape, bf), V(framed, f32), V(turned, f32), V(turned, bf),
            V(turned, bf), V(rim, bf), V(rim, bf), V((2, owned, every), bf),
            V((batches, GROUP * height, width), f32), V((batches, GROUP * height, width), f32),
            V((KW * KW, channels, width), f32), V((batches, channels, width), f32),
            V((padded, 128), f32), V((24, padded), f32), V((spots, 24, padded), f32),
            V((8, padded), f32), V((8, lanes), f32), V((128, padded), f32),
            V((owned, every), f32), V((owned, every), f32),
            dma((4,)), dma((3,)), dma((2,)), dma((2,)), dma((2,)),
            dma((2, 2)), dma((2, 2)),
            dma((spots,)), dma((spots,)), dma((spots,)), dma((spots,)),
            dma((2,)), dma((2,)), dma((peers,)), dma((peers,)), dma((1,)),
        ],
        compiler_params=pltpu.CompilerParams(
            vmem_limit_bytes=60 * 1024 * 1024, collective_id=ident, has_side_effects=True
        ),
        cost_estimate=pl.CostEstimate(
            flops=2 * KW * KW * batches * channels * height * width,
            bytes_accessed=30 * batches * channels * height * width,
            transcendentals=0,
        ),
    )(crop, x, cot, ocean, kernel, scales, expand_t, shrink, uplift, offset)


def chunks_of(total, size):
    return [(start, min(size, total - start)) for start in range(0, total, size)]


def nt(a, b):
    return lax.dot_general(a, b, (((1,), (1,)), ((), ())), preferred_element_type=jnp.float32)


def nn(a, b):
    return jnp.dot(a, b, preferred_element_type=jnp.float32)


def mlp_body(
    pin_ref, back_ref, et_ref, w_ref, up_ref, off_ref,
    res_ref, dn_ref, ge_out, gw_out, gu_out, go_out,
    pin, pint, back, backt, res_acc, dn_acc, ge, gw, gu, go,
):
    m = pl.program_id(0)
    last = pl.num_programs(0) - 1
    rows, channels, width = pin_ref.shape[1:]
    hidden = et_ref.shape[0]
    for r in range(rows):
        cols = slice(r * width, (r + 1) * width)
        value = pin_ref[0, r]
        pin[:, cols] = value
        pint[cols, :] = value.T
        value = back_ref[0, r]
        back[:, cols] = value
        backt[cols, :] = value.T

    @pl.when(m == 0)
    def _():
        ge[...] = jnp.zeros_like(ge)
        gw[...] = jnp.zeros_like(gw)
        gu[...] = jnp.zeros_like(gu)
        go[...] = jnp.zeros_like(go)

    go[...] += jnp.sum(backt[...].astype(jnp.float32), axis=0, keepdims=True)
    for index, (start, size) in enumerate(chunks_of(hidden, 512)):
        span = slice(start, start + size)
        et = et_ref[span, :]
        wt = w_ref[span, :]
        hid = nt(pint[...], et) + up_ref[:, span]
        dact = nt(backt[...], wt)
        square = hid * hid
        inner = GELU_A * hid * (1.0 + GELU_B * square)
        t = jnp.tanh(inner)
        half = 0.5 * (1.0 + t)
        act = (hid * half).astype(jnp.bfloat16)
        slope = half + 0.5 * hid * (1.0 - t * t) * (GELU_A * (1.0 + 3.0 * GELU_B * square))
        dhid = (slope * dact).astype(jnp.bfloat16)
        res_part = nn(act, wt)
        dn_part = nn(dhid, et)
        if index == 0:
            res_acc[...] = res_part
            dn_acc[...] = dn_part
        else:
            res_acc[...] += res_part
            dn_acc[...] += dn_part
        ge[:, span] += nn(pin[...], dhid)
        gw[:, span] += nn(back[...], act)
        gu[:, span] += jnp.sum(dhid.astype(jnp.float32), axis=0, keepdims=True)

        @pl.when(m == last)
        def _():
            ge_out[span, :] = ge[:, span].astype(jnp.bfloat16).T
            gw_out[span, :] = gw[:, span].astype(jnp.bfloat16).T

    for r in range(rows):
        cols = slice(r * width, (r + 1) * width)
        res_ref[0, r] = (res_acc[cols, :] + off_ref[...]).astype(jnp.bfloat16).T
        dn_ref[0, r] = dn_acc[cols, :].astype(jnp.bfloat16).T

    @pl.when(m == last)
    def _():
        gu_out[...] = gu[...]
        go_out[...] = go[...]


def mlp(pin, back, expand_t, shrink, uplift, offset):
    batches, rows, channels, width = pin.shape
    hidden = expand_t.shape[0]
    pixels = rows * width
    block = pl.BlockSpec((1, rows, channels, width), lambda m: (m, 0, 0, 0))
    whole = lambda shape: pl.BlockSpec(shape, lambda m: (0, 0), pipeline_mode=pl.Buffered(1))
    bf, f32 = jnp.bfloat16, jnp.float32
    return pl.pallas_call(
        mlp_body,
        grid=(batches,),
        in_specs=[
            block, block,
            whole((hidden, channels)), whole((hidden, channels)),
            whole((1, hidden)), whole((1, channels)),
        ],
        out_specs=[
            block, block,
            whole((hidden, channels)), whole((hidden, channels)),
            whole((1, hidden)), whole((1, channels)),
        ],
        out_shape=[
            jax.ShapeDtypeStruct(pin.shape, bf),
            jax.ShapeDtypeStruct(pin.shape, bf),
            jax.ShapeDtypeStruct((hidden, channels), bf),
            jax.ShapeDtypeStruct((hidden, channels), bf),
            jax.ShapeDtypeStruct((1, hidden), f32),
            jax.ShapeDtypeStruct((1, channels), f32),
        ],
        scratch_shapes=[
            pltpu.VMEM((channels, pixels), bf),
            pltpu.VMEM((pixels, channels), bf),
            pltpu.VMEM((channels, pixels), bf),
            pltpu.VMEM((pixels, channels), bf),
            pltpu.VMEM((pixels, channels), f32),
            pltpu.VMEM((pixels, channels), f32),
            pltpu.VMEM((channels, hidden), f32),
            pltpu.VMEM((channels, hidden), f32),
            pltpu.VMEM((1, hidden), f32),
            pltpu.VMEM((1, channels), f32),
        ],
        compiler_params=pltpu.CompilerParams(vmem_limit_bytes=62 * 1024 * 1024),
        cost_estimate=pl.CostEstimate(
            flops=12 * batches * pixels * channels * hidden,
            bytes_accessed=2 * 4 * channels * hidden,
            transcendentals=batches * pixels * hidden,
        ),
    )(pin, back, expand_t, shrink, uplift, offset)


def mlp_fused_body(
    normed, back_hbm, et_hbm, w_hbm, bias_ref,
    res_out, dn_out, share_ref, low_ref, small_ref, pair_in, first_in, second_in,
    up_ref, off_ref, gu_ref, go_ref, line, land, land_back, stage, et_ref, w_ref,
    pin, pint, back, backt, res_acc, dn_acc, act_all, dhid_all,
    in_send, in_recv, out_send, out_recv, load_sem, own_sem, keep_sem,
    pair_send, pair_recv, first_send, first_recv, second_send, second_recv, fetch_sem,
    pass_send, pass_recv, relay_send, relay_recv,
):
    f32, bf = jnp.float32, jnp.bfloat16
    batches, height, channels, width = normed.shape
    peers = lax.axis_size("lvl")
    me = lax.axis_index("lvl")
    rows = height // peers
    pixels = rows * width
    hidden = et_ref.shape[0]
    spots = lax.axis_size("sp")
    spot = lax.axis_index("sp")
    chips = spots // 2
    chip, core = spot // 2, lax.rem(spot, 2)
    owned = hidden // spots
    across, along, diagonal = chip_neighbours(chip)
    near = (across, along)
    sibling = spot + 1 - 2 * core
    mine = (2 * across + core, 2 * along + core, 2 * diagonal + core)
    others = (2 * across + 1 - core, 2 * along + 1 - core, 2 * diagonal + 1 - core)
    mesh_id = pl.DeviceIdType.MESH
    weights = ((et_hbm, et_ref), (w_hbm, w_ref))

    def owner_rows(owner):
        return pl.ds(pl.multiple_of(owner * owned, 16), owned)

    def weight_load(which, k):
        owner = (mine[0], mine[1], spot, sibling)[k]
        return pltpu.make_async_copy(
            weights[which][0].at[owner], weights[which][1].at[owner_rows(owner), :],
            load_sem.at[which, k],
        )

    def weight_pass(which, k, owner):
        rows_now = owner_rows(owner)
        source = weights[which][1].at[rows_now, :] if k == 2 else weights[which][0].at[owner]
        return pltpu.make_async_remote_copy(
            src_ref=source, dst_ref=weights[which][1].at[rows_now, :],
            send_sem=pass_send.at[which, k], recv_sem=pass_recv.at[which, k],
            device_id={"sp": sibling}, device_id_type=mesh_id,
        )

    def relay(which, owner):
        return pltpu.make_async_remote_copy(
            src_ref=weights[which][0].at[owner], dst_ref=weights[which][1].at[owner_rows(owner), :],
            send_sem=relay_send.at[which], recv_sem=relay_recv.at[which],
            device_id={"sp": mine[which]}, device_id_type=mesh_id,
        )

    load_back = pltpu.make_async_copy(back_hbm, land_back, own_sem.at[batches])
    load_back.start()
    for which in range(2):
        for k in range(4):
            weight_load(which, k).start()

    barrier = pltpu.get_barrier_semaphore()
    for k in range(1, peers):
        pl.semaphore_signal(
            barrier, inc=1, device_id={"lvl": lax.rem(me + k, peers)}, device_id_type=mesh_id
        )
    pl.semaphore_signal(barrier, inc=1, device_id={"sp": sibling}, device_id_type=mesh_id)
    for k in range(3):
        pl.semaphore_signal(barrier, inc=1, device_id={"sp": mine[k]}, device_id_type=mesh_id)
    pl.semaphore_wait(barrier, peers - 1 + 4)

    def span_of(at):
        return pl.ds(pl.multiple_of(at * channels, 8), channels)

    def in_copy(m, k):
        to = lax.rem(me + k, peers)
        return pltpu.make_async_remote_copy(
            src_ref=normed.at[m, pl.ds(to * rows, rows)],
            dst_ref=land.at[m, :, span_of(me), :],
            send_sem=in_send.at[m, k], recv_sem=in_recv.at[m, k],
            device_id={"lvl": to}, device_id_type=mesh_id,
        )

    def own_in(m):
        return pltpu.make_async_copy(
            normed.at[m, pl.ds(me * rows, rows)], land.at[m, :, span_of(me), :], own_sem.at[m]
        )

    outs = (res_out, dn_out)

    def out_copy(m, k, which):
        to = lax.rem(me + k, peers)
        return pltpu.make_async_remote_copy(
            src_ref=stage.at[which, m, :, span_of(to), :],
            dst_ref=outs[which].at[m, pl.ds(me * rows, rows)],
            send_sem=out_send.at[which, m, k], recv_sem=out_recv.at[which, m, k],
            device_id={"lvl": to}, device_id_type=mesh_id,
        )

    def own_out(m, which):
        return pltpu.make_async_copy(
            stage.at[which, m, :, span_of(me), :],
            outs[which].at[m, pl.ds(me * rows, rows)],
            keep_sem.at[which, m],
        )

    for m in range(batches):
        own_in(m).start()
    for k in range(1, peers):
        in_copy(0, k).start()
    for which in range(2):
        relay(which, mine[1 - which]).start()
        for k in range(2):
            weight_pass(which, k, mine[k]).start()
    for s in range(spots):
        row = bias_ref[s]
        up_ref[:, s * owned : (s + 1) * owned] = row[0:1, :owned]
        each = off_ref.shape[1] // spots
        off_ref[:, s * each : (s + 1) * each] = row[1:2, :each]
    gu_ref[...] = jnp.zeros_like(gu_ref)
    go_ref[...] = jnp.zeros_like(go_ref)
    load_back.wait()
    for which in range(2):
        relay(which, mine[1 - which]).wait_send()
        relay(which, mine[2]).wait_recv()
        weight_pass(which, 2, mine[2]).start()
    for which in range(2):
        for k in range(4):
            weight_load(which, k).wait()
        for k in range(2):
            weight_pass(which, k, mine[k]).wait_send()
            weight_pass(which, k, others[k]).wait_recv()
    for which in range(2):
        weight_pass(which, 2, mine[2]).wait_send()
        weight_pass(which, 2, others[2]).wait_recv()

    spans = chunks_of(hidden, 512)

    def one(m, carry):
        own_in(m).wait()
        for k in range(1, peers):
            in_copy(m, k).wait()

        @pl.when(m == 0)
        def _():
            for other in range(1, batches):
                for k in range(1, peers):
                    in_copy(other, k).start()

        mine_now = pl.ds(pl.multiple_of(m * pixels, 128), pixels)
        for r in range(rows):
            here = slice(r * width, (r + 1) * width)
            cols = pl.ds(pl.multiple_of(m * pixels + r * width, 128), width)
            value = land[m, r]
            pin[:, cols] = value
            pint[here, :] = value.T
            value = land_back[m, r]
            back[:, cols] = value
            backt[here, :] = value.T
        go_ref[...] += jnp.sum(backt[...].astype(f32), axis=0, keepdims=True)
        for index, (start, size) in enumerate(spans):
            span = slice(start, start + size)
            et = et_ref[span, :]
            wt = w_ref[span, :]
            hid = nt(pint[...], et) + up_ref[:, span]
            dact = nt(backt[...], wt)
            square = hid * hid
            half = 0.5 + 0.5 * jnp.tanh(hid * (GELU_A + (GELU_A * GELU_B) * square))
            full = hid * half
            act = full.astype(bf)
            slope = half + full * (1.0 - half) * (
                2.0 * GELU_A + (6.0 * GELU_A * GELU_B) * square
            )
            dhid = (slope * dact).astype(bf)
            act_all[mine_now, span] = act
            dhid_all[mine_now, span] = dhid
            res_part = nn(act, wt)
            dn_part = nn(dhid, et)
            if index == 0:
                res_acc[...] = res_part
                dn_acc[...] = dn_part
            else:
                res_acc[...] += res_part
                dn_acc[...] += dn_part
            gu_ref[:, span] += jnp.sum(dhid.astype(f32), axis=0, keepdims=True)

        for r in range(rows):
            here = slice(r * width, (r + 1) * width)
            stage[0, m, r] = (res_acc[here, :] + off_ref[...]).astype(bf).T
            stage[1, m, r] = dn_acc[here, :].astype(bf).T
        for which in range(2):
            for k in range(1, peers):
                out_copy(m, k, which).start()
            own_out(m, which).start()
        return carry

    lax.fori_loop(0, batches, one, 0)

    grads = (et_ref, w_ref)

    def pair_copy(which, q):
        return pltpu.make_async_remote_copy(
            src_ref=grads[which].at[owner_rows(2 * q + 1 - core), :],
            dst_ref=pair_in.at[which, q],
            send_sem=pair_send.at[which, q], recv_sem=pair_recv.at[which, q],
            device_id={"sp": sibling}, device_id_type=mesh_id,
        )

    def spare(which, q):
        return grads[which].at[owner_rows(2 * q + 1 - core), :]

    def fetch(which, source, q, slot):
        return pltpu.make_async_copy(source, spare(which, q), fetch_sem.at[which, slot])

    def first_copy(which, slot):
        owner = (2 * diagonal + core, 2 * near[which] + core)[slot]
        return pltpu.make_async_remote_copy(
            src_ref=grads[which].at[owner_rows(owner), :], dst_ref=first_in.at[which, slot],
            send_sem=first_send.at[which, slot], recv_sem=first_recv.at[which, slot],
            device_id={"sp": 2 * near[which] + core}, device_id_type=mesh_id,
        )

    def second_copy(which):
        owner = 2 * near[1 - which] + core
        return pltpu.make_async_remote_copy(
            src_ref=grads[which].at[owner_rows(owner), :], dst_ref=second_in.at[which],
            send_sem=second_send.at[which], recv_sem=second_recv.at[which],
            device_id={"sp": owner}, device_id_type=mesh_id,
        )

    strip = 16

    def add_rows(which, to, source):
        def add(i, carry):
            at = pl.ds(pl.multiple_of(to * owned + i * strip, 16), strip)
            more = pl.ds(pl.multiple_of(source * owned + i * strip, 16), strip)
            total = grads[which][at, :].astype(f32) + grads[which][more, :].astype(f32)
            grads[which][at, :] = total.astype(bf)
            return carry

        lax.fori_loop(0, owned // strip, add, 0)

    def fold_pair(q):
        for which in range(2):
            pair_copy(which, q).wait()
            fetch(which, pair_in.at[which, q], q, q).start()
        for which in range(2):
            fetch(which, pair_in.at[which, q], q, q).wait()
            add_rows(which, 2 * q + core, 2 * q + 1 - core)

            @pl.when(diagonal == q)
            def _():
                first_copy(which, 0).start()

            @pl.when(near[which] == q)
            def _():
                first_copy(which, 1).start()

    waiting = []
    for start, size in spans:
        span = slice(start, start + size)
        et_ref[span, :] = nn(pin[...], dhid_all[:, span]).astype(bf).T
        w_ref[span, :] = nn(back[...], act_all[:, span]).astype(bf).T
        ready = [q for q in range(chips) if start < 2 * (q + 1) * owned <= start + size]
        for q in ready:
            for which in range(2):
                pair_copy(which, q).start()
        for q in waiting:
            fold_pair(q)
        waiting = ready
    for q in waiting:
        fold_pair(q)
    for which in range(2):
        first_copy(which, 0).wait()
        fetch(which, first_in.at[which, 0], 0, chips).start()
        fetch(which, first_in.at[which, 0], 0, chips).wait()
        add_rows(which, 2 * near[1 - which] + core, 1 - core)
        second_copy(which).start()
    for which in range(2):
        first_copy(which, 1).wait()
        fetch(which, first_in.at[which, 1], 1, chips + 1).start()
    for which in range(2):
        fetch(which, first_in.at[which, 1], 1, chips + 1).wait()
        second_copy(which).wait()
        fetch(which, second_in.at[which], 2, chips + 2).start()
    for which in range(2):
        fetch(which, second_in.at[which], 2, chips + 2).wait()

        def gather(i, carry, which=which):
            total = None
            for owner in (spot, 3 - core, 5 - core):
                at = pl.ds(pl.multiple_of(owner * owned + i * strip, 16), strip)
                value = grads[which][at, :].astype(f32)
                total = value if total is None else total + value
            at = pl.ds(pl.multiple_of(which * owned + i * strip, 16), strip)
            share_ref[at, :] = total
            low_ref[at, :] = total.astype(bf)
            return carry

        lax.fori_loop(0, owned // strip, gather, 0)
    piece = small_ref.shape[1]
    each = off_ref.shape[1] // spots
    line[...] = jnp.zeros_like(line)
    for s in range(spots):
        line[:, :owned] = gu_ref[:, s * owned : (s + 1) * owned]
        line[:, owned : owned + each] = go_ref[:, s * each : (s + 1) * each]
        for n in range(small_ref.shape[0] // spots):
            at = n * spots + s
            small_ref[at : at + 1, :] = line[:, n * piece : (n + 1) * piece]
    for m in range(batches):
        for which in range(2):
            own_out(m, which).wait()
            for k in range(1, peers):
                out_copy(m, k, which).wait()


def mlp_fused(normed, back, expand_t, shrink, bias, lines, padded, ident):
    batches, height, channels, width = normed.shape
    peers = lax.axis_size("lvl")
    rows = height // peers
    spots, owned, every = expand_t.shape
    hidden = spots * owned
    chips = spots // 2
    pixels = rows * width
    bf, f32 = jnp.bfloat16, jnp.float32
    hbm = pl.BlockSpec(memory_space=pl.ANY)
    vmem = pl.BlockSpec(memory_space=pltpu.VMEM)
    dma = pltpu.SemaphoreType.DMA
    V, S = pltpu.VMEM, jax.ShapeDtypeStruct
    landing = (batches, rows, every, width)
    return pl.pallas_call(
        mlp_fused_body,
        in_specs=[hbm, hbm, hbm, hbm, vmem],
        out_specs=[hbm, hbm, vmem, vmem, vmem, hbm, hbm, hbm],
        out_shape=[
            S(normed.shape, bf), S(normed.shape, bf),
            S((2 * owned, every), f32), S((2 * owned, every), bf), S((lines, padded), f32),
            S((2, chips, owned, every), bf), S((2, 2, owned, every), bf),
            S((2, owned, every), bf),
        ],
        scratch_shapes=[
            V((1, hidden), f32), V((1, every), f32), V((1, hidden), f32), V((1, every), f32),
            V((1, lines // spots * padded), f32),
            V(landing, bf), V(landing, bf), V((2,) + landing, bf),
            V((hidden, every), bf), V((hidden, every), bf),
            V((every, batches * pixels), bf), V((pixels, every), bf),
            V((every, batches * pixels), bf), V((pixels, every), bf),
            V((pixels, every), f32), V((pixels, every), f32),
            V((batches * pixels, hidden), bf), V((batches * pixels, hidden), bf),
            dma((batches, peers)), dma((batches, peers)),
            dma((2, batches, peers)), dma((2, batches, peers)),
            dma((2, 4)), dma((batches + 1,)), dma((2, batches)),
            dma((2, chips)), dma((2, chips)), dma((2, 2)), dma((2, 2)), dma((2,)), dma((2,)),
            dma((2, chips + 3)), dma((2, 3)), dma((2, 3)), dma((2,)), dma((2,)),
        ],
        compiler_params=pltpu.CompilerParams(
            vmem_limit_bytes=63 * 1024 * 1024, collective_id=ident, has_side_effects=True
        ),
        cost_estimate=pl.CostEstimate(
            flops=12 * batches * pixels * every * hidden,
            bytes_accessed=8 * every * hidden,
            transcendentals=batches * pixels * hidden,
        ),
    )(normed, back, expand_t, shrink, bias)[:5]


def finish_body(
    conv_hbm, xt_hbm, dn_hbm, share_hbm, low_hbm, small_ref, par_ref, mask_ref, k_ref,
    igrad_hbm, zfull, zrecv_hbm, kg_ref, tot_ref, own_ref,
    conv, xt, dn, frame, obuf, taps, acc49, part, coef, stat, stat_all, kcols, msg, srecv,
    kmsg, krecv, zown, zlow, zrecv, zsmall, zsrecv, ztot,
    load_sem, out_sem, s_send, s_recv, k_send, k_recv, h_send, h_recv,
    z_send, z_recv, g_send, g_recv, q_send, q_recv, f_sem,
):
    f32, bf = jnp.float32, jnp.bfloat16
    batches, height, channels, width = conv.shape
    groups = channels // GROUP
    peers, place = lax.axis_size("lvl"), lax.axis_index("lvl")
    spots, spot = lax.axis_size("sp"), lax.axis_index("sp")
    mesh_id = pl.DeviceIdType.MESH

    pairs = [(dn_hbm, dn), (conv_hbm, conv)]
    loads = [
        [
            pltpu.make_async_copy(src.at[m], dst.at[m], load_sem.at[n, m])
            for n, (src, dst) in enumerate(pairs)
        ]
        for m in range(batches)
    ]
    load_x = pltpu.make_async_copy(xt_hbm, xt, load_sem.at[2, 0])
    for batch_loads in loads:
        for load in batch_loads:
            load.start()
    load_x.start()

    barrier = pltpu.get_barrier_semaphore()
    for k in range(1, peers):
        pl.semaphore_signal(
            barrier, inc=1, device_id={"lvl": lax.rem(place + k, peers)}, device_id_type=mesh_id
        )
    for k in range(1, spots):
        pl.semaphore_signal(
            barrier, inc=1, device_id={"sp": lax.rem(spot + k, spots)}, device_id_type=mesh_id
        )

    quarter = share_hbm.shape[0] // peers

    def quarter_rows(at):
        return pl.ds(pl.multiple_of(at * quarter, 8), quarter)

    def z_copy(k):
        to = lax.rem(place + k, peers)
        return pltpu.make_async_remote_copy(
            src_ref=low_hbm.at[quarter_rows(to), :], dst_ref=zrecv_hbm.at[k],
            send_sem=z_send.at[k], recv_sem=z_recv.at[k],
            device_id={"lvl": to}, device_id_type=mesh_id,
        )

    def g_copy(k):
        return pltpu.make_async_remote_copy(
            src_ref=zlow, dst_ref=zfull.at[quarter_rows(place), :],
            send_sem=g_send.at[k], recv_sem=g_recv.at[k],
            device_id={"lvl": lax.rem(place + k, peers)}, device_id_type=mesh_id,
        )

    def g_wait(k):
        source = lax.rem(place + peers - k, peers)
        pltpu.make_async_remote_copy(
            src_ref=zlow, dst_ref=zfull.at[quarter_rows(source), :],
            send_sem=g_send.at[k], recv_sem=g_recv.at[k],
            device_id={"lvl": lax.rem(place + k, peers)}, device_id_type=mesh_id,
        ).wait()

    def spread_copy(src, dst, send, recv, k):
        return pltpu.make_async_remote_copy(
            src_ref=src, dst_ref=dst.at[k], send_sem=send.at[k], recv_sem=recv.at[k],
            device_id={"sp": lax.rem(spot + k, spots)}, device_id_type=mesh_id,
        )

    def q_copy(k):
        return pltpu.make_async_remote_copy(
            src_ref=zsmall, dst_ref=zsrecv.at[k], send_sem=q_send.at[k], recv_sem=q_recv.at[k],
            device_id={"lvl": lax.rem(place + k, peers)}, device_id_type=mesh_id,
        )

    def to_next():
        return pltpu.make_async_remote_copy(
            src_ref=frame.at[:, pl.ds(height, MARGIN)], dst_ref=frame.at[:, pl.ds(0, MARGIN)],
            send_sem=h_send.at[0], recv_sem=h_recv.at[0],
            device_id={"sp": lax.rem(spot + 1, spots)}, device_id_type=mesh_id,
        )

    def to_prev():
        return pltpu.make_async_remote_copy(
            src_ref=frame.at[:, pl.ds(MARGIN, MARGIN)],
            dst_ref=frame.at[:, pl.ds(MARGIN + height, MARGIN)],
            send_sem=h_send.at[1], recv_sem=h_recv.at[1],
            device_id={"sp": lax.rem(spot + spots - 1, spots)}, device_id_type=mesh_id,
        )

    def load_own():
        return pltpu.make_async_copy(share_hbm.at[quarter_rows(place), :], zown, f_sem.at[0])

    def load_part(k):
        return pltpu.make_async_copy(zrecv_hbm.at[k], zrecv.at[k], f_sem.at[k])

    def keep_own():
        return pltpu.make_async_copy(zlow, zfull.at[quarter_rows(place), :], f_sem.at[peers])

    load_own().start()
    pl.semaphore_wait(barrier, peers - 1 + spots - 1)
    for k in range(1, peers):
        z_copy(k).start()

    def slot_sum(ref, own):
        total = None
        for source in range(spots):
            k = lax.rem(spot - source + spots, spots)
            value = ref[k]
            total = value if total is None else total + value
        return total

    stat[...] = jnp.zeros_like(stat)
    kcols[...] = jnp.zeros_like(kcols)
    lane = lax.broadcasted_iota(jnp.int32, (channels, 128), 1)
    every_row = (channels, width)

    def column(ref, at):
        return jnp.broadcast_to(ref[:channels, at : at + 1], every_row)

    for m in range(batches):
        coef[m, 0] = column(par_ref, m)
    for m in range(batches):
        for load in loads[m]:
            load.wait()

        def sums(g, carry, m=m):
            now = pl.ds(pl.multiple_of(g * GROUP, GROUP), GROUP)
            mean = coef[m, 0, now, :]
            plain, cross = None, None
            for i in range(height):
                grad = dn[m, i, now, :].astype(f32)
                turn = grad * (conv[m, i, now, :] - mean)
                plain = grad if plain is None else plain + grad
                cross = turn if cross is None else cross + turn
            part[0, m, now, :] = plain
            part[1, m, now, :] = cross
            return carry

        lax.fori_loop(0, groups, sums, 0)
    tile = jnp.zeros((channels, 128), f32)
    for m in range(batches):
        plain = jnp.sum(part[0, m], axis=1, keepdims=True)
        cross = jnp.sum(part[1, m], axis=1, keepdims=True) * par_ref[:channels, 8 + m : 9 + m]
        tile = jnp.where(lane == m, plain, tile)
        tile = jnp.where(lane == batches + m, cross, tile)
    stat[:channels, :] = tile
    head = 8
    msg[:head, :] = stat[...].T[:head, :]
    msg[head:, :] = small_ref[...]
    srecv[0] = msg[...]
    for k in range(1, spots):
        spread_copy(msg, srecv, s_send, s_recv, k).start()

    masks = lane_tap_masks(width)
    fill_taps(k_ref, taps, masks, groups)
    for k in range(1, spots):
        spread_copy(msg, srecv, s_send, s_recv, k).wait()
    total = slot_sum(srecv, msg)
    tot_ref[...] = total[:head, :]
    zsmall[...] = total[head:, :]
    for k in range(1, peers):
        q_copy(k).start()
    padded = jnp.concatenate(
        [total[:head, :], jnp.zeros((128 - head, total.shape[1]), f32)], axis=0
    )
    stat_all[...] = padded.T

    gain = column(par_ref, 24)
    for m in range(batches):
        rho = column(par_ref, 8 + m)
        lead = rho * gain
        share = lead * column(par_ref, 16 + m)
        coef[m, 1] = lead
        coef[m, 2] = column(stat_all, m) * share
        coef[m, 3] = column(stat_all, batches + m) * rho * share

    def grad_rows(m, now, wanted):
        mean, lead = coef[m, 0, now, :], coef[m, 1, now, :]
        flat, tilt = coef[m, 2, now, :], coef[m, 3, now, :]
        for i in wanted:
            off = (conv[m, i, now, :] - mean) * tilt + flat
            frame[m, MARGIN + i, now, :] = (
                lead * dn[m, i, now, :].astype(f32) - mask_ref[m, i : i + 1, :] * off
            )

    edges = list(range(MARGIN)) + list(range(height - MARGIN, height))

    def rims(g, carry):
        now = pl.ds(pl.multiple_of(g * GROUP, GROUP), GROUP)
        for m in range(batches):
            grad_rows(m, now, edges)
        return carry

    lax.fori_loop(0, groups, rims, 0)

    @pl.when(spot < spots - 1)
    def _():
        to_next().start()

    @pl.when(spot > 0)
    def _():
        to_prev().start()

    load_x.wait()

    def weight_terms(g, carry):
        now = pl.ds(pl.multiple_of(g * GROUP, GROUP), GROUP)
        for t in range(KW * KW):
            acc49[t, now, :] = jnp.zeros((GROUP, width), f32)

        def one(m, inner):
            grad_rows(m, now, range(MARGIN, height - MARGIN))
            for base in range(0, height, ROWS):
                back = [frame[m, MARGIN + base + i, now, :] for i in range(ROWS)]
                for b in range(KW):
                    rolled = [
                        shifted(xt[m, base + r, now, :], b - MARGIN)
                        for r in range(ROWS + KW - 1)
                    ]
                    for a in range(KW):
                        total = None
                        for i in range(ROWS):
                            term = back[i] * rolled[i + a]
                            total = term if total is None else total + term
                        acc49[a * KW + b, now, :] += total
            return inner

        lax.fori_loop(0, batches, one, 0)
        return carry

    middle = groups
    lax.fori_loop(0, middle, weight_terms, 0)
    load_own().wait()
    for k in range(1, peers):
        z_copy(k).wait()
        load_part(k).start()
    for k in range(1, peers):
        load_part(k).wait()

    def fold(i, carry):
        at = pl.ds(pl.multiple_of(i * GROUP, 8), GROUP)
        total = zown[at, :]
        for k in range(1, peers):
            total = total + zrecv[k, at, :].astype(f32)
        zlow[at, :] = total.astype(bf)
        return carry

    lax.fori_loop(0, quarter // GROUP, fold, 0)
    for k in range(1, peers):
        g_copy(k).start()
    keep_own().start()
    lax.fori_loop(middle, groups, weight_terms, 0)
    wide_lane = lax.broadcasted_iota(jnp.int32, (channels, width), 1)

    def reduce_tap(t, carry):
        b = lax.rem(t, KW) - MARGIN
        kept = jnp.logical_and(wide_lane + b >= 0, wide_lane + b < width)
        summed = jnp.sum(jnp.where(kept, acc49[t], 0.0), axis=1, keepdims=True)
        kcols[:channels, :] = jnp.where(lane == t, summed, kcols[:channels, :])
        return carry

    lax.fori_loop(0, KW * KW, reduce_tap, 0)
    kmsg[...] = kcols[...].T[: kmsg.shape[0], :]
    krecv[0] = kmsg[...]
    for k in range(1, spots):
        spread_copy(kmsg, krecv, k_send, k_recv, k).start()


    @pl.when(spot < spots - 1)
    def _():
        to_next().wait_send()
        to_prev().wait_recv()

    @pl.when(spot > 0)
    def _():
        to_prev().wait_send()
        to_next().wait_recv()

    @pl.when(spot == 0)
    def _():
        frame[:, :MARGIN] = jnp.zeros((batches, MARGIN, channels, width), f32)

    @pl.when(spot == spots - 1)
    def _():
        frame[:, MARGIN + height :] = jnp.zeros((batches, MARGIN, channels, width), f32)

    def save(m):
        return pltpu.make_async_copy(obuf.at[m], igrad_hbm.at[m], out_sem.at[m])

    def inputs(m, carry):
        def one(g, inner):
            now = pl.ds(pl.multiple_of(g * GROUP, GROUP), GROUP)
            for base in range(0, height, ROWS):
                outs = depthwise_rows(
                    lambda r: frame[m, base + r, now, :], taps, now, ROWS, -1
                )
                for i in range(ROWS):
                    obuf[m, base + i, now, :] = outs[i].astype(bf)
            return inner

        lax.fori_loop(0, groups, one, 0)
        save(m).start()
        return carry

    lax.fori_loop(0, batches, inputs, 0)
    for k in range(1, spots):
        spread_copy(kmsg, krecv, k_send, k_recv, k).wait()
    kg_ref[...] = slot_sum(krecv, kmsg)
    for k in range(1, peers):
        q_copy(k).wait()
    zsrecv[0] = zsmall[...]
    total = None
    for source in range(peers):
        value = zsrecv[lax.rem(place - source + peers, peers)]
        total = value if total is None else total + value
    ztot[...] = total
    own_ref[...] = jnp.zeros_like(own_ref)
    piece = small_ref.shape[1]
    for n in range(small_ref.shape[0] // spots):
        own_ref[0:1, n * piece : (n + 1) * piece] = ztot[pl.ds(n * spots + spot, 1), :]
    keep_own().wait()
    for k in range(1, peers):
        g_wait(k)
    for m in range(batches):
        save(m).wait()


def finish(conv, xt, dn, share, low, small, params, mask_cells, kernel, ident):
    batches, height, channels, width = conv.shape
    bf, f32 = jnp.bfloat16, jnp.float32
    peers, spots = lax.axis_size("lvl"), lax.axis_size("sp")
    padded = -(-channels // 128) * 128
    taps = -(-(KW * KW) // 8) * 8
    head = 8
    lines = small.shape[0]
    every = share.shape[1]
    quarter = share.shape[0] // peers
    hbm = pl.BlockSpec(memory_space=pl.ANY)
    vmem = pl.BlockSpec(memory_space=pltpu.VMEM)
    dma = pltpu.SemaphoreType.DMA
    framed = (batches, height + 2 * MARGIN, channels, width)
    S = jax.ShapeDtypeStruct
    return pl.pallas_call(
        finish_body,
        in_specs=[hbm] * 5 + [vmem] * 4,
        out_specs=[hbm, hbm, hbm, vmem, vmem, vmem],
        out_shape=[
            S(conv.shape, bf),
            S(share.shape, bf), S((peers, quarter, every), bf),
            S((taps, padded), f32), S((head, padded), f32), S((8, lines // spots * padded), f32),
        ],
        scratch_shapes=[
            pltpu.VMEM(conv.shape, f32), pltpu.VMEM(framed, f32),
            pltpu.VMEM(conv.shape, bf), pltpu.VMEM(framed, f32), pltpu.VMEM(conv.shape, bf),
            pltpu.VMEM((KW * KW, channels, width), f32),
            pltpu.VMEM((KW * KW, channels, width), f32),
            pltpu.VMEM((2, batches, channels, width), f32),
            pltpu.VMEM((batches, 4, channels, width), f32),
            pltpu.VMEM((padded, 128), f32), pltpu.VMEM((padded, 128), f32),
            pltpu.VMEM((padded, 128), f32),
            pltpu.VMEM((head + lines, padded), f32),
            pltpu.VMEM((spots, head + lines, padded), f32),
            pltpu.VMEM((taps, padded), f32),
            pltpu.VMEM((spots, taps, padded), f32),
            pltpu.VMEM((quarter, every), f32), pltpu.VMEM((quarter, every), bf),
            pltpu.VMEM((peers, quarter, every), bf),
            pltpu.VMEM(small.shape, f32),
            pltpu.VMEM((peers,) + small.shape, f32), pltpu.VMEM(small.shape, f32),
            dma((3, batches)), dma((batches,)), dma((spots,)), dma((spots,)), dma((spots,)), dma((spots,)),
            dma((2,)), dma((2,)), dma((peers,)), dma((peers,)), dma((peers,)), dma((peers,)),
            dma((peers,)), dma((peers,)), dma((peers + 1,)),
        ],
        compiler_params=pltpu.CompilerParams(
            vmem_limit_bytes=60 * 1024 * 1024, collective_id=ident, has_side_effects=True
        ),
        cost_estimate=pl.CostEstimate(
            flops=4 * KW * KW * batches * channels * height * width,
            bytes_accessed=34 * batches * channels * height * width,
            transcendentals=0,
        ),
    )(conv, xt, dn, share, low, small, params, mask_cells, kernel)


RATES = {"kernel": 0.15, "scales": 0.2, "expand": 0.035, "uplift": 0.1, "shrink": 0.018, "offset": 0.1}


def close_body(
    crop, step, x_ref, cot_ref, res_ref, dx_ref, mask_ref, ge_ref, gs_ref,
    e_ref, e1_ref, e2_ref, s_ref, s1_ref, s2_ref,
    kg_ref, tot_ref, own_ref,
    k_ref, k1_ref, k2_ref, c_ref, c1_ref, c2_ref, u_ref, u1_ref, u2_ref, o_ref, o1_ref, o2_ref,
    out_ref, igrad_ref, eg_out, em_out, en_out, sg_out, sm_out, sn_out,
    kg_out, km_out, kn_out, cg_out, cm_out, cn_out, ug_out, um_out, un_out, og_out, om_out, on_out,
    scr, scx,
):
    f32 = jnp.float32
    batches, block, height, width = x_ref.shape
    time = jnp.full((8, 128), step[0] + 1, jnp.int32).astype(f32)
    one = 1.0 / (1.0 - jnp.exp(time * math.log(beta_one)))[0:1, 0:1]
    two = 1.0 / (1.0 - jnp.exp(time * math.log(beta_two)))[0:1, 0:1]

    def step_of(weight, first, second, grad, rate):
        first_new = beta_one * first + (1.0 - beta_one) * grad
        second_new = beta_two * second + (1.0 - beta_two) * grad * grad
        update = first_new * one / (jnp.sqrt(second_new * two) + epsilon) + weight_decay * weight
        return second_new, weight - rate * update

    @pl.when(pl.program_id(0) == 0)
    def _():
        taps, channels = k_ref.shape
        kg = kg_ref[:taps, :channels]
        kg_out[...] = kg
        km_out[...], kn_out[...] = step_of(
            k_ref[...], k1_ref[...], k2_ref[...], kg, RATES["kernel"]
        )
        tot = tot_ref[...]
        plain = jnp.sum(tot[:batches], axis=0, keepdims=True)[:, :channels]
        cross = jnp.sum(tot[batches : 2 * batches], axis=0, keepdims=True)[:, :channels]
        for row, grad in ((0, cross), (1, plain)):
            at = slice(row, row + 1)
            cg_out[at, :] = grad
            cm_out[at, :], cn_out[at, :] = step_of(
                c_ref[at, :], c1_ref[at, :], c2_ref[at, :], grad, RATES["scales"]
            )
        owned, each = u_ref.shape[1], o_ref.shape[1]
        ug = own_ref[0:1, :owned]
        ug_out[...] = ug
        um_out[...], un_out[...] = step_of(
            u_ref[...], u1_ref[...], u2_ref[...], ug, RATES["uplift"]
        )
        og = own_ref[0:1, owned : owned + each]
        og_out[...] = og
        om_out[...], on_out[...] = step_of(
            o_ref[...], o1_ref[...], o2_ref[...], og, RATES["offset"]
        )

    strip = 16

    def rows(i, carry):
        at = pl.ds(pl.multiple_of(i * strip, strip), strip)
        for g_ref, w, w1, w2, g_out, m_out, n_out, rate in (
            (ge_ref, e_ref, e1_ref, e2_ref, eg_out, em_out, en_out, RATES["expand"]),
            (gs_ref, s_ref, s1_ref, s2_ref, sg_out, sm_out, sn_out, RATES["shrink"]),
        ):
            grad = g_ref[at, :].astype(f32)
            g_out[at, :] = grad
            m_out[at, :], n_out[at, :] = step_of(w[at, :], w1[at, :], w2[at, :], grad, rate)
        return carry

    lax.fori_loop(0, ge_ref.shape[0] // strip, rows, 0)
    row = lax.broadcasted_iota(jnp.int32, (height, width), 0)

    def cells(g, carry):
        c0 = pl.multiple_of(g * GROUP, GROUP)
        now = pl.ds(c0, GROUP)
        for m in range(batches):
            keep = (row < crop[m]).astype(f32)
            mask = mask_ref[m]
            for i in range(height):
                at = slice(i * GROUP, (i + 1) * GROUP)
                scr[m, at, :] = res_ref[m, i, now, :].astype(f32)
                scx[m, at, :] = dx_ref[m, i, now, :].astype(f32)
            for c in range(GROUP):
                part = pl.ds(c, height, stride=GROUP)
                out_ref[m, c0 + c] = mask * (x_ref[m, c0 + c].astype(f32) + scr[m, part, :])
                dres = cot_ref[m, c0 + c].astype(f32) * mask
                igrad_ref[m, c0 + c] = keep * (dres + scx[m, part, :])
        return carry

    lax.fori_loop(0, block // GROUP, cells, 0)


def close(crop, step, x, cot, res, dx, mask_cells, shares, expand, shrink, kg, tot, own, kernel, scales, uplift, offset):
    batches, channels, height, width = x.shape
    f32 = jnp.float32
    owned, every = expand[0].shape
    block = CLOSE_BLOCK
    steps = channels // block
    part = owned // steps
    natural = pl.BlockSpec((batches, block, height, width), lambda i: (0, i, 0, 0))
    turned = pl.BlockSpec((batches, height, block, width), lambda i: (0, 0, i, 0))
    smem = pl.BlockSpec(memory_space=pltpu.SMEM)
    lines = pl.BlockSpec((part, every), lambda i: (i, 0))
    later = pl.BlockSpec((part, every), lambda i: (i + steps, 0))

    def whole(v):
        zeros = (0,) * v.ndim
        return pl.BlockSpec(v.shape, lambda i: zeros)

    S = jax.ShapeDtypeStruct
    small = list(kernel) + list(scales) + list(uplift) + list(offset)
    return pl.pallas_call(
        close_body,
        grid=(steps,),
        in_specs=[smem, smem, natural, natural, turned, turned, whole(mask_cells), lines, later]
        + [lines] * 6 + [whole(v) for v in (kg, tot, own)] + [whole(v) for v in small],
        out_specs=[natural, natural] + [lines] * 6 + [whole(v) for v in small],
        out_shape=[S(x.shape, f32)] * 2 + [S((owned, every), f32)] * 6
        + [S(v.shape, f32) for v in small],
        scratch_shapes=[
            pltpu.VMEM((batches, GROUP * height, width), f32),
            pltpu.VMEM((batches, GROUP * height, width), f32),
        ],
        compiler_params=pltpu.CompilerParams(vmem_limit_bytes=63 * 1024 * 1024),
    )(
        crop, step, x, cot, res, dx, mask_cells, shares, shares,
        *expand, *shrink, kg, tot, own, *small,
    )


def sums_body(xt_ref, res_ref, dn_ref, conv_ref, mask_ref, par_ref, out_ref, stat_ref, scr):
    batches, height = res_ref.shape[:2]
    width = res_ref.shape[3]

    def one(m, stats):
        lane = lax.broadcasted_iota(jnp.int32, (GROUP, 128), 1)
        mean = jnp.sum(jnp.where(lane == m, par_ref[...], 0.0), axis=1, keepdims=True)
        rho = jnp.sum(jnp.where(lane == batches + m, par_ref[...], 0.0), axis=1, keepdims=True)
        mean = jnp.broadcast_to(mean, (GROUP, width))
        rho = jnp.broadcast_to(rho, (GROUP, width))
        plain = jnp.zeros((GROUP, width), jnp.float32)
        cross = jnp.zeros((GROUP, width), jnp.float32)
        for i in range(height):
            grad = dn_ref[m, i].astype(jnp.float32)
            plain = plain + grad
            cross = cross + grad * ((conv_ref[m, i] - mean) * rho)
            value = xt_ref[m, MARGIN + i] + res_ref[m, i].astype(jnp.float32)
            scr[pl.ds(i, GROUP, stride=height), :] = value * mask_ref[m, i : i + 1, :]
        for c in range(GROUP):
            out_ref[m, c] = scr[c * height : (c + 1) * height, :]
        stats = jnp.where(lane == m, jnp.sum(plain, axis=1, keepdims=True), stats)
        return jnp.where(lane == batches + m, jnp.sum(cross, axis=1, keepdims=True), stats)

    stat_ref[...] = lax.fori_loop(0, batches, one, jnp.zeros((GROUP, 128), jnp.float32))


def output_and_sums(xt, res, dn, conv, mask_cells, params):
    batches, height, channels, width = res.shape
    turned = lambda rows: pl.BlockSpec((batches, rows, GROUP, width), lambda g: (0, 0, g, 0))
    return pl.pallas_call(
        sums_body,
        grid=(pl.cdiv(channels, GROUP),),
        in_specs=[
            turned(height + 2 * MARGIN),
            turned(height), turned(height), turned(height),
            pl.BlockSpec((batches, height, width), lambda g: (0, 0, 0)),
            pl.BlockSpec((GROUP, 128), lambda g: (g, 0)),
        ],
        out_specs=[
            pl.BlockSpec((batches, GROUP, height, width), lambda g: (0, g, 0, 0)),
            pl.BlockSpec((GROUP, 128), lambda g: (g, 0)),
        ],
        out_shape=[
            jax.ShapeDtypeStruct((batches, channels, height, width), jnp.float32),
            jax.ShapeDtypeStruct((channels, 128), jnp.float32),
        ],
        scratch_shapes=[pltpu.VMEM((GROUP * height, width), jnp.float32)],
        cost_estimate=pl.CostEstimate(
            flops=10 * batches * channels * height * width,
            bytes_accessed=20 * batches * channels * height * width,
            transcendentals=0,
        ),
    )(xt, res, dn, conv, mask_cells, params)


def conv_back_body(
    crop, xt_ref, grad_ref, up_ref, dn_ref, cot_ref, k_ref, mask_ref,
    out_ref, kg_ref, scr, wscr, frame, sums,
):
    batches, height = grad_ref.shape[:2]
    width = grad_ref.shape[3]
    masks = lane_tap_masks(width)
    for a in range(KW):
        for b in range(KW):
            t = a * KW + b
            spread = jnp.broadcast_to(k_ref[:, t : t + 1], (GROUP, width))
            wscr[t] = jnp.where(masks[KW - 1 - b], spread, 0.0)
            sums[t] = jnp.zeros((GROUP, width), jnp.float32)

    def one(m, carry):
        for r in range(MARGIN):
            frame[r] = up_ref[m, r]
            frame[MARGIN + height + r] = dn_ref[m, r]
        for i in range(height):
            frame[MARGIN + i] = grad_ref[m, i]
        for base in range(0, height, ROWS):
            for b in range(KW):
                rolled = [
                    shifted(xt_ref[m, base + r], b - MARGIN) for r in range(ROWS + KW - 1)
                ]
                for a in range(KW):
                    part = None
                    for i in range(ROWS):
                        term = frame[MARGIN + base + i] * rolled[i + a]
                        part = term if part is None else part + term
                    sums[a * KW + b] += part
            acc = [None] * ROWS
            for b in range(KW):
                rolled = [
                    shifted(frame[base + r], MARGIN - b) for r in range(ROWS + KW - 1)
                ]
                for a in range(KW):
                    tap = wscr[a * KW + b]
                    for i in range(ROWS):
                        term = tap * rolled[i + KW - 1 - a]
                        acc[i] = term if acc[i] is None else acc[i] + term
            for i in range(ROWS):
                scr[pl.ds(base + i, GROUP, stride=height), :] = acc[i]
        row = lax.broadcasted_iota(jnp.int32, (height, width), 0)
        for c in range(GROUP):
            dres = cot_ref[m, c].astype(jnp.float32) * mask_ref[m]
            total = dres + scr[c * height : (c + 1) * height, :]
            out_ref[m, c] = jnp.where(row < crop[m, 0], total, 0.0)
        return carry

    lax.fori_loop(0, batches, one, 0)
    columns = []
    for t in range(KW * KW):
        kept = jnp.where(masks[t % KW], sums[t], 0.0)
        columns.append((t, jnp.sum(kept, axis=1, keepdims=True)))
    kg_ref[...] = put_columns(columns)


def conv_backward(crop, xt, grad_conv, up, down, cot, kernel, mask_cells):
    batches, height, channels, width = grad_conv.shape
    natural = pl.BlockSpec((batches, GROUP, height, width), lambda g, c: (0, g, 0, 0))
    turned = lambda rows: pl.BlockSpec((batches, rows, GROUP, width), lambda g, c: (0, 0, g, 0))
    return pl.pallas_call(
        conv_back_body,
        grid_spec=pltpu.PrefetchScalarGridSpec(
            num_scalar_prefetch=1,
            grid=(pl.cdiv(channels, GROUP),),
            in_specs=[
                turned(height + 2 * MARGIN),
                turned(height),
                turned(MARGIN), turned(MARGIN),
                natural,
                pl.BlockSpec((GROUP, KW * KW), lambda g, c: (g, 0)),
                pl.BlockSpec((batches, height, width), lambda g, c: (0, 0, 0)),
            ],
            out_specs=[natural, pl.BlockSpec((GROUP, 128), lambda g, c: (g, 0))],
            scratch_shapes=[
                pltpu.VMEM((GROUP * height, width), jnp.float32),
                pltpu.VMEM((KW * KW, GROUP, width), jnp.float32),
                pltpu.VMEM((height + 2 * MARGIN, GROUP, width), jnp.float32),
                pltpu.VMEM((KW * KW, GROUP, width), jnp.float32),
            ],
        ),
        out_shape=[
            jax.ShapeDtypeStruct((batches, channels, height, width), jnp.float32),
            jax.ShapeDtypeStruct((channels, 128), jnp.float32),
        ],
        cost_estimate=pl.CostEstimate(
            flops=4 * KW * KW * batches * channels * height * width,
            bytes_accessed=14 * batches * channels * height * width,
            transcendentals=0,
        ),
    )(crop, xt, grad_conv, up, down, cot, kernel, mask_cells)


def neighbours(head, tail, axis):
    count = lax.axis_size(axis)
    up = lax.ppermute(tail, axis, [(i, i + 1) for i in range(count - 1)])
    down = lax.ppermute(head, axis, [(i + 1, i) for i in range(count - 1)])
    return up, down


def aligned(channels, height, owned, levels):
    return (
        channels % 8 == 0 and height % levels == 0 and height == ROWS
        and owned % 16 == 0 and (2 * owned) % (8 * levels) == 0
        and channels % CLOSE_BLOCK == 0 and owned % (16 * (channels // CLOSE_BLOCK)) == 0
    )


def on_device(
    input_field, cotangent, ocean_mask, crop_rows, step_count,
    kernel, kernel_first, kernel_second,
    scales, scales_first, scales_second,
    expand, expand_first, expand_second,
    uplift, uplift_first, uplift_second,
    shrink, shrink_first, shrink_second,
    offset, offset_first, offset_second,
):
    f32, bf = jnp.float32, jnp.bfloat16
    batches, channels, height, width = input_field.shape
    sp = lax.axis_size("sp")
    lvl = lax.axis_size("lvl")
    place = lax.axis_index("sp")
    owned = uplift.shape[0]
    hidden, every = sp * owned, sp * offset.shape[0]
    if aligned(channels, height, owned, lvl) and sp == 8:
        crop = crop_rows.reshape(batches)
        (
            conv, xt, normed, pixel_back, expand_all, shrink_all, params, mask_cells, bias, turned_k,
        ) = forward(
            crop, input_field, cotangent, ocean_mask, kernel.T, scales,
            expand.T, shrink, uplift[None], offset[None], 0,
        )
        padded = params.shape[0]
        lines = -(-(owned + offset.shape[0]) // padded) * sp
        result, grad_normed, share, low, small = mlp_fused(
            normed, pixel_back, expand_all, shrink_all, bias, lines, padded, 1
        )
        field_grad, shares, _, kernel_rows, both, own = finish(
            conv, xt, grad_normed, share, low, small, params, mask_cells, turned_k, 2
        )
        (
            block_output, input_grad, eg, em, en, sg, sm, sn,
            kg, km, kn, cg, cm, cn, ug, um, un, og, om, on,
        ) = close(
            crop, step_count.reshape(1), input_field, cotangent, result, field_grad, mask_cells,
            shares, (expand.T, expand_first.T, expand_second.T),
            (shrink, shrink_first, shrink_second), kernel_rows, both, own,
            (kernel.T, kernel_first.T, kernel_second.T), (scales, scales_first, scales_second),
            (uplift[None], uplift_first[None], uplift_second[None]),
            (offset[None], offset_first[None], offset_second[None]),
        )
        return (
            block_output, input_grad, kg.T, km.T, kn.T, cg, cm, cn, eg.T, em.T, en.T,
            ug[0], um[0], un[0], sg, sm, sn, og[0], om[0], on[0], step_count + 1,
        )
    else:
        expand_all = lax.all_gather(expand.T.astype(bf), "sp", axis=0, tiled=True)
        shrink_all = lax.all_gather(shrink.astype(bf), "sp", axis=0, tiled=True)
        uplift_all = lax.all_gather(uplift.astype(bf), "sp", axis=0, tiled=True)
        offset_all = lax.all_gather(offset.astype(bf), "sp", axis=0, tiled=True)

        valid = (jnp.arange(height, dtype=jnp.int32)[None, :] < crop_rows).astype(f32)
        mask_cells = ocean_mask.astype(f32) * valid[:, :, None]
        valid_low = valid.astype(bf)[:, None, :, None]
        head = input_field[:, :, :MARGIN] * valid_low[:, :, :MARGIN]
        tail = input_field[:, :, height - MARGIN :] * valid_low[:, :, height - MARGIN :]
        up, down = neighbours(head.transpose(0, 2, 1, 3), tail.transpose(0, 2, 1, 3), "sp")
        conv, xt, dres, stats = conv_forward(
            crop_rows, input_field, cotangent, up, down, kernel, mask_cells
        )
        every = lax.all_gather(stats[:, : 4 * batches], "sp", axis=0)
        sums = every[:, :, :batches]
        squares = every[:, :, batches : 2 * batches]
        cells = every[:, :, 2 * batches : 3 * batches]
        count = jnp.maximum(jnp.sum(cells, axis=0), 1.0)
        mean = jnp.sum(sums, axis=0) / count
        gap = sums / jnp.maximum(cells, 1.0) - mean[None]
        variance = jnp.sum(squares + cells * gap * gap, axis=0) / count
        rho = lax.rsqrt(variance + 1e-05)

        def spread(stat):
            return stat.T[:, None, :, None]

        gain = scales[0][None, None, :, None]
        shift = scales[1][None, None, :, None]
        normed = ((conv - spread(mean)) * spread(rho) * gain + shift).astype(bf)

        def to_pixels(v):
            return lax.all_to_all(v, "lvl", split_axis=1, concat_axis=2, tiled=True)

        def to_channels(v):
            return lax.all_to_all(v, "lvl", split_axis=2, concat_axis=1, tiled=True)

        pixel_back = to_pixels(dres)
        biases = (uplift_all.astype(f32)[None], offset_all.astype(f32)[None])
        result, grad_normed, grad_expand, grad_shrink, grad_uplift, grad_offset = mlp(
            to_pixels(normed), pixel_back, expand_all, shrink_all, *biases
        )
        result = to_channels(result)
        grad_normed = to_channels(grad_normed)
        params = jnp.concatenate([mean, rho], axis=1)
        params = jnp.pad(params, ((0, 0), (0, 128 - params.shape[1])))
        block_output, local = output_and_sums(xt, result, grad_normed, conv, mask_cells, params)
        both = lax.psum(local[:, : 2 * batches], "sp")
        plain, cross = both[:, :batches], both[:, batches:]
        scales_grad = jnp.stack([jnp.sum(cross, axis=1), jnp.sum(plain, axis=1)], axis=0)
        whitened = (conv - spread(mean)) * spread(rho)
        grad_conv = spread(rho) * (
            gain * grad_normed.astype(f32)
            - mask_cells[:, :, None, :] * gain * (spread(plain) + whitened * spread(cross)) / spread(count)
        )
        back_up, back_down = neighbours(
            grad_conv[:, :MARGIN], grad_conv[:, height - MARGIN :], "sp"
        )
        input_grad, kernel_cols = conv_backward(
            crop_rows, xt, grad_conv, back_up, back_down, cotangent, kernel, mask_cells
        )
        kernel_grad = lax.psum(kernel_cols[:, : KW * KW], "sp")

        def own_share(partial):
            rows = partial.shape[0] // sp
            parts = lax.all_to_all(
                partial.reshape(sp, rows, partial.shape[1]), "sp", split_axis=0, concat_axis=0
            )
            share = jnp.sum(parts.astype(f32), axis=0).astype(bf)
            return jnp.sum(lax.all_gather(share, "lvl", axis=0).astype(f32), axis=0)

        share_expand = own_share(grad_expand)
        share_shrink = own_share(grad_shrink)
        small = lax.psum(
            jnp.concatenate([grad_uplift[0], grad_offset[0]]), ("sp", "lvl")
        )
    share_uplift = lax.dynamic_slice_in_dim(small, place * owned, owned)
    share_offset = lax.dynamic_slice_in_dim(
        small, hidden + place * offset.shape[0], offset.shape[0]
    )
    step_float = (step_count + 1).astype(f32)
    kernel_moment, kernel_next = adamw(
        kernel, kernel_first, kernel_second, kernel_grad, 0.15, step_float
    )
    scales_moment, scales_next = adamw(
        scales, scales_first, scales_second, scales_grad, 0.2, step_float
    )
    expand_grad = share_expand.T
    expand_moment, expand_next = adamw(
        expand, expand_first, expand_second, expand_grad, 0.035, step_float
    )
    uplift_moment, uplift_next = adamw(
        uplift, uplift_first, uplift_second, share_uplift, 0.1, step_float
    )
    shrink_moment, shrink_next = adamw(
        shrink, shrink_first, shrink_second, share_shrink, 0.018, step_float
    )
    offset_moment, offset_next = adamw(
        offset, offset_first, offset_second, share_offset, 0.1, step_float
    )
    return (
        block_output, input_grad,
        kernel_grad, kernel_moment, kernel_next,
        scales_grad, scales_moment, scales_next,
        expand_grad, expand_moment, expand_next,
        share_uplift, uplift_moment, uplift_next,
        share_shrink, shrink_moment, shrink_next,
        share_offset, offset_moment, offset_next,
        step_count + 1,
    )


def solution(mesh):
    tile = P(None, "lvl", "sp", None)
    by_channel = P("lvl", None)
    by_scale = P(None, "lvl")
    by_hidden = P(None, "sp")
    by_row = P("sp", None)
    line = P("sp")
    in_specs = (
        tile, tile, P(None, "sp", None), P(None, "sp"), P(),
        by_channel, by_channel, by_channel,
        by_scale, by_scale, by_scale,
        by_hidden, by_hidden, by_hidden,
        line, line, line,
        by_row, by_row, by_row,
        line, line, line,
    )
    out_specs = (
        tile, tile,
        by_channel, by_channel, by_channel,
        by_scale, by_scale, by_scale,
        by_hidden, by_hidden, by_hidden,
        line, line, line,
        by_row, by_row, by_row,
        line, line, line,
        P(),
    )
    return jax.shard_map(
        on_device, mesh=mesh, in_specs=in_specs, out_specs=out_specs, check_vma=False
    )
```

profile of v0, /device:TPU:30, one launch (start us, length us, event | category | flops | bytes accessed | tf_op | source)
XLA Modules:
  0.0 320.2 jit_solution(17622806871859967774)
XLA Ops:
  0.7 59.7 %shard_map.382 = (f32[3,16,200,128]{3,2,1,0:T(8,128)}, f32[3,22,200,128]{3,2,1,0:T(8,128)}, bf16[3,16,200,128]{3,2,1,0:T(8,128)(2,1)}, bf16[3,4,800,128]{3,2,1,0...) custom-call(s32[3]{0:T(128)} %bitcast.39, ...), custom_call_target="tpu_custom_call" | custom-call | flops 120422400 | bytes 36864000 | tf_op jit(solution)/shard_map/pallas_call | solution.py:541
  60.3 170.3 %shard_map.383 = (bf16[3,16,200,128]{3,2,1,0:T(8,128)(2,1)}, bf16[3,16,200,128]{3,2,1,0:T(8,128)(2,1)}, f32[800,800]{1,0:T(8,128)}, bf16[800,800]{1,0:T(8,128)(2...) custom-call(bf16[3,16,200,128]{3,2,1,0:T(8,128)(2,1)} %get-tuple-ele, ...), custom_call_target="tpu_custom_call" | custom-call | flops 47185920000 | bytes 20480000 | tf_op jit(solution)/shard_map/pallas_call | solution.py:1034
  230.7 70.7 %shard_map.384 = (bf16[3,16,200,128]{3,2,1,0:T(8,128)(2,1)}, bf16[800,800]{1,0:T(8,128)(2,1)}, bf16[4,200,800]{2,1,0:T(8,128)(2,1)}, f32[56,256]{1,0:T(8,128)}, f32[8,256]{1,0:T(8,128)}, /*index=5*/f32[8,512]{1,0:T(8,128)}) custom-call(f32[3,16,200,128]{3,2,1,0:T(8,128)} %get-tuple-element.67.conv_hbm, f32[3,22,200,128]{3,2,1,0:T(8,128)} %get-tuple-element.68.xt_hbm, ...), custom_call_target="tpu_custom_call" | custom-call | flops 240844800 | bytes 41779200 | tf_op jit(solution)/shard_map/pallas_call | solution.py:1417
  302.0 17.0 %shard_map.385 = (f32[3,200,16,128]{3,2,1,0:T(8,128)}, f32[3,200,16,128]{3,2,1,0:T(8,128)}, f32[400,800]{1,0:T(8,128)}, f32[400,800]{1,0:T(8,128)}, f32[400,800]...) custom-call(s32[3]{0:T(128)} %bitcast.40, ...), custom_call_target="tpu_custom_call" | custom-call | tf_op jit(solution)/shard_map/pallas_call | solution.py:1566
where the time goes:
time: 323 us; the launch traced here: 320 us
  Pallas kernels  318 us (98%)
    pallas_call x1, Pallas kernels, mlp_fused(): pl.pallas_call(mlp_fused_body, in_specs=[hbm, hbm, hbm, hbm, vmem], out_s...  170 us
    pallas_call x1, Pallas kernels, finish(): pl.pallas_call(finish_body, in_specs=[hbm] * 5 + [vmem] * 4, out_specs=[h...  70.7 us
    pallas_call x1, Pallas kernels, forward(): pl.pallas_call(forward_body, in_specs=[pl.BlockSpec(memory_space=pltpu.SM...  59.7 us
    pallas_call x1, Pallas kernels, close(): pl.pallas_call(close_body, grid=(steps,), in_specs=[smem, smem, natural,...  17 us

commit v1 on v0

--- a/solution.py
+++ b/solution.py
@@ -1508,7 +1508,7 @@
             o_ref[...], o1_ref[...], o2_ref[...], og, RATES["offset"]
         )
 
-    strip = 16
+    strip = ge_ref.shape[0]
 
     def rows(i, carry):
         at = pl.ds(pl.multiple_of(i * strip, strip), strip)

time: 323 us -> 323 us (level)
  no operation moved by 1% of the time
where the time goes in v1:
time: 323 us; the launch traced here: 320 us
  Pallas kernels  318 us (98%)
    pallas_call x1, Pallas kernels, mlp_fused(): pl.pallas_call(mlp_fused_body, in_specs=[hbm, hbm, hbm, hbm, vmem], out_s...  170 us
    pallas_call x1, Pallas kernels, finish(): pl.pallas_call(finish_body, in_specs=[hbm] * 5 + [vmem] * 4, out_specs=[h...  70.7 us
    pallas_call x1, Pallas kernels, forward(): pl.pallas_call(forward_body, in_specs=[pl.BlockSpec(memory_space=pltpu.SM...  59.7 us
    pallas_call x1, Pallas kernels, close(): pl.pallas_call(close_body, grid=(steps,), in_specs=[smem, smem, natural,...  17 us

profile of v1, /device:TPU:30, one launch (start us, length us, event | category | flops | bytes accessed | tf_op | source)
XLA Modules:
  0.0 320.1 jit_solution(6728375189235044842)
XLA Ops:
  0.7 59.7 %shard_map.382 = (f32[3,16,200,128]{3,2,1,0:T(8,128)}, f32[3,22,200,128]{3,2,1,0:T(8,128)}, bf16[3,16,200,128]{3,2,1,0:T(8,128)(2,1)}, bf16[3,4,800,128]{3,2,1,0...) custom-call(s32[3]{0:T(128)} %bitcast.39, ...), custom_call_target="tpu_custom_call" | custom-call | flops 120422400 | bytes 36864000 | tf_op jit(solution)/shard_map/pallas_call | solution.py:541
  60.3 170.3 %shard_map.383 = (bf16[3,16,200,128]{3,2,1,0:T(8,128)(2,1)}, bf16[3,16,200,128]{3,2,1,0:T(8,128)(2,1)}, f32[800,800]{1,0:T(8,128)}, bf16[800,800]{1,0:T(8,128)(2...) custom-call(bf16[3,16,200,128]{3,2,1,0:T(8,128)(2,1)} %get-tuple-ele, ...), custom_call_target="tpu_custom_call" | custom-call | flops 47185920000 | bytes 20480000 | tf_op jit(solution)/shard_map/pallas_call | solution.py:1034
  230.7 70.7 %shard_map.384 = (bf16[3,16,200,128]{3,2,1,0:T(8,128)(2,1)}, bf16[800,800]{1,0:T(8,128)(2,1)}, bf16[4,200,800]{2,1,0:T(8,128)(2,1)}, f32[56,256]{1,0:T(8,128)}, f32[8,256]{1,0:T(8,128)}, /*index=5*/f32[8,512]{1,0:T(8,128)}) custom-call(f32[3,16,200,128]{3,2,1,0:T(8,128)} %get-tuple-element.67.conv_hbm, f32[3,22,200,128]{3,2,1,0:T(8,128)} %get-tuple-element.68.xt_hbm, ...), custom_call_target="tpu_custom_call" | custom-call | flops 240844800 | bytes 41779200 | tf_op jit(solution)/shard_map/pallas_call | solution.py:1417
  302.0 17.0 %shard_map.385 = (f32[3,200,16,128]{3,2,1,0:T(8,128)}, f32[3,200,16,128]{3,2,1,0:T(8,128)}, f32[400,800]{1,0:T(8,128)}, f32[400,800]{1,0:T(8,128)}, f32[400,800]...) custom-call(s32[3]{0:T(128)} %bitcast.40, ...), custom_call_target="tpu_custom_call" | custom-call | tf_op jit(solution)/shard_map/pallas_call | solution.py:1566
